TPU v7x, 32 devices: a whole 2x2x4 slice. The times are simulated.
32 devices in a mesh: cfg: 4 (over z), mode: 8 (over y, x, core).
Axes of the slice: x: 2, y: 2, z: 4, core: 2. Of those that a mesh axis runs over, the one named last changes fastest.
Arguments:
- coords: bfloat16 [10368, 2048], P('mode', 'cfg'), may hold values from -6 to 6
- curvature: float32 [10368], P('mode'), may hold values from 0.2 to 5
- weight: float32 [10368], P('mode'), may hold values from 0.3 to 3
- polar: bfloat16 [10368, 10368], P('mode'), may hold values from -0.078125 to 0.078125
- forces: bfloat16 [10368, 2048], P('mode', 'cfg'), may hold values from -6 to 6
Outputs:
- gradient: float32 [10368, 10368], P('cfg', 'mode')
All inputs are finite; a program needn't handle non-finite values.
Results may differ from a plain program's by a relative error of at most 0.019.
Values may be sent and summed in bfloat16 or wider, within the bound.
A program may use at most 192 MiB of HBM per device.

v0:
```python
import math
import jax
import jax.numpy as jnp
from jax import lax
from jax.sharding import PartitionSpec as P


def on_device(coords, curvature, weight, polar, forces):
    f32 = jnp.float32
    bf16 = jnp.bfloat16
    configs_dev = coords.shape[1]
    scaled = (coords.astype(f32) * curvature[:, None]).astype(bf16)
    weighted = (coords.astype(f32) * weight[:, None]).astype(bf16)
    contract = (((0,), (0,)), ((), ()))
    shares = lax.psum_scatter(
        lax.dot_general(polar, scaled, contract, preferred_element_type=f32).astype(jnp.bfloat16),
        "mode",
        scatter_dimension=0,
        tiled=True,
    ).astype(jnp.float32)
    resid_rows = (forces.astype(f32) + shares).astype(bf16)
    residual = lax.all_gather(resid_rows, "mode", axis=0, tiled=True)
    factor = 1.0 / math.sqrt(configs_dev * lax.axis_size("cfg"))
    across = (((1,), (1,)), ((), ()))
    return lax.psum_scatter(
        (lax.dot_general(residual, weighted, across, preferred_element_type=f32) * factor).astype(
            jnp.bfloat16
        ),
        "cfg",
        scatter_dimension=0,
        tiled=True,
    ).astype(jnp.float32)


def solution(mesh):
    placed = (P("mode", "cfg"), P("mode"), P("mode"), P("mode", None), P("mode", "cfg"))
    return jax.shard_map(
        on_device, mesh=mesh, in_specs=placed, out_specs=P("cfg", "mode"), check_vma=False
    )
```

profile of v0, /device:TPU:0, one launch (start us, length us, event | category | flops | bytes accessed | tf_op | source)
XLA Modules:
  0.0 746.0 jit_solution(12773726648723765596)
XLA Ops:
  6.5 0.0 reduce-scatter.5.cloned.1.call-start
  6.5 23.2 %fusion = bf16[10368,512]{1,0:T(8,128)(2,1)} fusion(bf16[1296,10368]{1,0:T(8,128)(2,1)} %param.8, bf16[1296,512]{1,0:T(8,128)(2,1)} %param.5, f32[1296]{0:T(1024)} %param.6), kind=kOutput, calls=%fused_computation.2 | convolution fusion | flops 13766713344 | bytes 38822976 | tf_op jit(solution)/shard_map/dot_general | solution.py:16
  29.7 0.0 copy-start
  29.7 0.0 reduce-scatter.5.cloned.1.call-update
  29.7 0.0 copy-start.1
  29.7 0.0 copy-start.2
  29.7 0.0 all-gather.2.cloned.1.call-start
  29.8 85.4 %reduce-scatter.5.cloned.1.call-done = bf16[1296,512]{1,0:T(8,128)(2,1)} async-done(((bf16[10368,512]{1,0:T(8,128)(2,1)}), bf16[1296,512]{1,0:T(8,128)(2,1)}) %reduce-scatter.5.cloned.1.call-update) | async-done | bytes 1327120 | tf_op jit(solution)/shard_map/reduce_scatter | solution.py:15
  115.2 0.0 copy-done
  115.2 2.7 add_convert_fusion
  117.9 0.0 all-gather.2.cloned.1.call-update
  118.0 0.2 reduce-scatter.7.cloned.1.call-start
  118.2 63.6 %all-gather.2.cloned.1.call-done = bf16[10368,512]{1,0:T(8,128)(2,1)} async-done(((bf16[1296,512]{1,0:T(8,128)(2,1)}), bf16[10368,512]{1,0:T(8,128)(2,1)}) %all-gather.2.cloned.1.call-update) | async-done | bytes 10616848 | tf_op jit(solution)/shard_map/all_gather | solution.py:22
  181.8 0.0 copy-done.1
  181.8 0.0 copy-done.2
  181.8 22.4 %multiply_convert_fusion = bf16[10368,1296]{0,1:T(8,128)(2,1)} fusion(bf16[10368,512]{1,0:T(8,128)(2,1)} %all-gather.2.cloned.1.call-done, bf16[1296,512]{1,0:T(8,128)(2,1)S(1)} %copy-done.1, f32[1296]{0:T(1024)S(1)} %copy-done.2), kind=kOutput, calls=%fused_computation | convolution fusion | flops 13788278784 | bytes 38822976 | tf_op jit(solution)/shard_map/dot_general | solution.py:26
  204.2 35.9 %copy.6 = bf16[10368,1296]{1,0:T(8,128)(2,1)} copy(bf16[10368,1296]{0,1:T(8,128)(2,1)} %multiply_convert_fusion) | data formatting | bytes 53747712
  240.1 0.0 reduce-scatter.7.cloned.1.call-update
  240.2 479.6 %reduce-scatter.7.cloned.1.call-done = bf16[2592,1296]{1,0:T(8,128)(2,1)} async-done(((bf16[10368,1296]{1,0:T(8,128)(2,1)}), bf16[2592,1296]{1,0:T(8,128)(2,1)}) %reduce-scatter.7.cloned.1.call-update) | async-done | bytes 6718480
  719.7 10.6 %copy.7 = bf16[2592,1296]{0,1:T(8,128)(2,1)} copy(bf16[2592,1296]{1,0:T(8,128)(2,1)} %reduce-scatter.7.cloned.1.call-done) | data formatting | bytes 13436928
  730.4 9.1 %convert_element_type.40 = f32[2592,1296]{0,1:T(8,128)} convert(bf16[2592,1296]{0,1:T(8,128)(2,1)} %copy.7) | non-fusion elementwise | flops 3359232 | bytes 20155392 | tf_op jit(solution)/shard_map/convert_element_type | solution.py:32
Async XLA Ops:
  6.5 108.7 %reduce-scatter.5.cloned.1.call-start = ((), (), s32[]{:S(2)}) async-start(), calls=%async_computation.2 | async-start | bytes 11943936 | tf_op jit(solution)/shard_map/reduce_scatter | solution.py:15
  29.7 85.5 %copy-start = (bf16[1296,512]{1,0:T(8,128)(2,1)S(1)}, bf16[1296,512]{1,0:T(8,128)(2,1)}, u32[]{:S(2)}) copy-start(bf16[1296,512]{1,0:T(8,128)(2,1)} %param.9) | copy-start | bytes 3981316
  29.7 152.1 %copy-start.1 = (bf16[1296,512]{1,0:T(8,128)(2,1)S(1)}, bf16[1296,512]{1,0:T(8,128)(2,1)}, u32[]{:S(2)}) copy-start(bf16[1296,512]{1,0:T(8,128)(2,1)} %param.5) | copy-start | bytes 3981316
  29.7 152.1 %copy-start.2 = (f32[1296]{0:T(1024)S(1)}, f32[1296]{0:T(1024)}, u32[]{:S(2)}) copy-start(f32[1296]{0:T(1024)} %param.7) | copy-start | bytes 15556
  29.7 152.0 %all-gather.2.cloned.1.call-start = ((), (), s32[]{:S(2)}) async-start(), calls=%async_computation.3 | async-start | bytes 11943936 | tf_op jit(solution)/shard_map/all_gather | solution.py:22
  118.0 601.7 %reduce-scatter.7.cloned.1.call-start = ((), (), s32[]{:S(2)}) async-start(), calls=%async_computation.4 | async-start | bytes 36495360
Sparse Core Ops, SparseCore 0:
  29.8 85.3 reduce-scatter.4
  118.1 63.6 all-gather.1
  240.3 479.3 reduce-scatter.6
where the time goes:
time: 747 us; the launch traced here: 746 us
  waiting for transfers between devices  629 us (84%)
  local copies, waits for them, and re-layouts  46.6 us (6%)
  matrix products  45.6 us (6%)
  between operations  13.1 us (2%)
  other arithmetic  11.8 us (2%)
    unnamed x4, waiting for transfers between devices  480 us
    reduce_scatter x1, waiting for transfers between devices, on_device(): lax.psum_scatter(lax.dot_general(polar, scaled, contract, preferred_eleme...  85.4 us
    all_gather x1, waiting for transfers between devices, on_device(): residual = lax.all_gather(resid_rows, 'mode', axis=0, tiled=True)  63.6 us
    unnamed x8, local copies, waits for them, and re-layouts  46.6 us
    dot_general x1, matrix products, on_device(): lax.dot_general(polar, scaled, contract, preferred_element_type=f32)  23.2 us
    dot_general x1, matrix products, on_device(): lax.dot_general(residual, weighted, across, preferred_element_type=f32)  22.4 us
  transfers between devices with their start and end apart: 3, of which 3 were waited for; matrix products, arithmetic and copies ran while one was open for 0% of the time, Pallas kernels for 0%

commit v1 on v0

--- a/solution.py
+++ b/solution.py
@@ -3,6 +3,28 @@
 import jax.numpy as jnp
 from jax import lax
 from jax.sharding import PartitionSpec as P
+
+
+def laid_out(blocks, dim):
+    blocks = jnp.moveaxis(blocks, 0, dim)
+    lengths = blocks.shape
+    return blocks.reshape(*lengths[:dim], lengths[dim] * lengths[dim + 1], *lengths[dim + 2 :])
+
+
+def collected_by_bits(x, axis):
+    size = lax.axis_size(axis)
+    blocks = x[None]
+    for level in range(size.bit_length() - 1):
+        apart = 1 << level
+        partner_block = lax.ppermute(blocks, axis, [(i, i ^ apart) for i in range(size)])
+        both = jnp.stack([blocks, partner_block])
+        upper = lax.axis_index(axis) >> level & 1
+        blocks = jnp.where(upper == 0, both, both[::-1]).reshape(-1, *x.shape)
+    return blocks
+
+
+def gather_by_bits(x, axis, dim):
+    return laid_out(collected_by_bits(x, axis), dim)
 
 
 def on_device(coords, curvature, weight, polar, forces):
@@ -19,7 +41,7 @@
         tiled=True,
     ).astype(jnp.float32)
     resid_rows = (forces.astype(f32) + shares).astype(bf16)
-    residual = lax.all_gather(resid_rows, "mode", axis=0, tiled=True)
+    residual = gather_by_bits(resid_rows, "mode", 0)
     factor = 1.0 / math.sqrt(configs_dev * lax.axis_size("cfg"))
     across = (((1,), (1,)), ((), ()))
     return lax.psum_scatter(

time: 747 us -> 918 us (1.23)
  waiting for transfers between devices: 629 us -> 739 us
  local copies, waits for them, and re-layouts: 46.6 us -> 83.6 us
  other arithmetic: 11.8 us -> 30.5 us
    ppermute x0 -> x3, waiting for transfers between devices: none -> 176 us  [collected_by_bits(): lax.ppermute(blocks, axis, [(i, i ^ apart) for i in range(size)])]
    reduce_scatter x1 -> x0, waiting for transfers between devices: 85.4 us -> none  [on_device(): lax.psum_scatter(lax.dot_general(polar, scaled, contract, preferred_eleme...]
    unnamed x4, waiting for transfers between devices: 480 us -> 563 us
    all_gather x1 -> x0, waiting for transfers between devices: 63.6 us -> none  [on_device(): residual = lax.all_gather(resid_rows, 'mode', axis=0, tiled=True)]
    unnamed x8 -> x15, local copies, waits for them, and re-layouts: 46.6 us -> 64.8 us
    another operation x0 -> x5, other arithmetic: none -> 12.4 us  [collected_by_bits(): both = jnp.stack([blocks, partner_block])]
  transfers between devices with their start and end apart: 3 -> 5, of which waited for: 3 -> 5; matrix products, arithmetic and copies ran while one was open for 0% -> 0% of each run, Pallas kernels for 0% -> 0%
where the time goes in v1:
time: 918 us; the launch traced here: 916 us
  waiting for transfers between devices  739 us (81%)
  local copies, waits for them, and re-layouts  83.6 us (9%)
  matrix products  46.3 us (5%)
  other arithmetic  30.5 us (3%)
  between operations  13.5 us (1%)
    unnamed x4, waiting for transfers between devices  563 us
    ppermute x3, waiting for transfers between devices, collected_by_bits(): lax.ppermute(blocks, axis, [(i, i ^ apart) for i in range(size)])  176 us
    unnamed x15, local copies, waits for them, and re-layouts  64.8 us
    dot_general x1, matrix products, on_device(): lax.dot_general(polar, scaled, contract, preferred_element_type=f32)  23.9 us
    dot_general x1, matrix products, on_device(): lax.dot_general(residual, weighted, across, preferred_element_type=f32)  22.4 us
  transfers between devices with their start and end apart: 5, of which 5 were waited for; matrix products, arithmetic and copies ran while one was open for 0% of the time, Pallas kernels for 0%

profile of v1, /device:TPU:0, one launch (start us, length us, event | category | flops | bytes accessed | tf_op | source)
XLA Modules:
  0.0 916.1 jit_solution(14061544266081663681)
XLA Ops:
  6.5 23.9 %fusion = bf16[10368,512]{0,1:T(8,128)(2,1)} fusion(bf16[1296,10368]{1,0:T(8,128)(2,1)} %param.8, bf16[1296,512]{1,0:T(8,128)(2,1)} %param.5, f32[1296]{0:T(1024)} %param.6), kind=kOutput, calls=%fused_computation.3 | convolution fusion | flops 13766713344 | bytes 38822976 | tf_op jit(solution)/shard_map/dot_general | solution.py:38
  30.4 14.5 %copy.17 = bf16[10368,512]{1,0:T(8,128)(2,1)} copy(bf16[10368,512]{0,1:T(8,128)(2,1)} %fusion) | data formatting | bytes 21233664
  44.9 0.0 reduce-scatter.7.cloned.1.call-update
  45.0 0.2 reduce-scatter.9.cloned.1.call-start
  45.2 1.1 copy-done.2
  46.2 0.8 copy.10
  47.1 83.4 %reduce-scatter.7.cloned.1.call-done = bf16[1296,512]{1,0:T(8,128)(2,1)} async-done(((bf16[10368,512]{1,0:T(8,128)(2,1)}), bf16[1296,512]{1,0:T(8,128)(2,1)}) %reduce-scatter.7.cloned.1.call-update) | async-done | bytes 1327120
  130.4 1.8 copy.18
  132.2 1.9 fusion.10
  134.2 1.7 copy.11
  135.9 0.1 collective-permute-start
  136.0 3.2 collective-permute-done
  139.2 1.8 copy.12
  141.0 0.3 pad_maximum_fusion.2
  141.3 2.2 fusion.4
  143.5 2.7 copy.13
  146.2 1.5 collective-permute-start.1
  147.6 58.5 %collective-permute-done.1 = bf16[2,1296,512]{2,1,0:T(8,128)(2,1)} collective-permute-done((bf16[2,1296,512]{2,1,0:T(8,128)(2,1)}, bf16[2,1296,512]{2,1,0:T(8,128)(2,1)}, u32[]{:S(2)}, u32[]{:S(2)}) %collective-permute-start.1) | collective-permute-done | bytes 2654240 | tf_op jit(solution)/shard_map/ppermute | solution.py:19
  206.1 4.5 copy.14
  210.6 2.4 pad_maximum_fusion.1
  213.0 3.7 reverse_select_fusion.1
  216.8 8.0 copy.15
  224.8 1.5 collective-permute-start.2
  226.3 114.5 %collective-permute-done.2 = bf16[4,1296,512]{2,1,0:T(8,128)(2,1)} collective-permute-done((bf16[4,1296,512]{2,1,0:T(8,128)(2,1)}, bf16[4,1296,512]{2,1,0:T(8,128)(2,1)}, u32[]{:S(2)}, u32[]{:S(2)}) %collective-permute-start.2) | collective-permute-done | bytes 5308448 | tf_op jit(solution)/shard_map/ppermute | solution.py:19
  340.8 5.5 pad_maximum_fusion
  346.3 5.3 reverse_select_fusion
  351.6 22.4 %multiply_convert_fusion = bf16[10368,1296]{0,1:T(8,128)(2,1)} fusion(bf16[10368,512]{1,0:T(8,128)(2,1)} %bitcast.23, bf16[1296,512]{1,0:T(8,128)(2,1)S(1)} %copy-done.3, f32[1296]{0:T(1024)S(1)} %copy-done.4), kind=kOutput, calls=%fused_computation | convolution fusion | flops 13788278784 | bytes 38822976 | tf_op jit(solution)/shard_map/dot_general | solution.py:48
  374.0 35.9 %copy.19 = bf16[10368,1296]{1,0:T(8,128)(2,1)} copy(bf16[10368,1296]{0,1:T(8,128)(2,1)} %multiply_convert_fusion) | data formatting | bytes 53747712
  410.0 0.0 reduce-scatter.9.cloned.1.call-update
  410.0 479.5 %reduce-scatter.9.cloned.1.call-done = bf16[2592,1296]{1,0:T(8,128)(2,1)} async-done(((bf16[10368,1296]{1,0:T(8,128)(2,1)}), bf16[2592,1296]{1,0:T(8,128)(2,1)}) %reduce-scatter.9.cloned.1.call-update) | async-done | bytes 6718480
  889.5 10.7 %copy.20 = bf16[2592,1296]{0,1:T(8,128)(2,1)} copy(bf16[2592,1296]{1,0:T(8,128)(2,1)} %reduce-scatter.9.cloned.1.call-done) | data formatting | bytes 13436928
  900.2 9.1 convert_element_type.40
  (10 shorter events, 0.0 us)
Async XLA Ops:
  6.5 123.9 %reduce-scatter.7.cloned.1.call-start = ((), (), s32[]{:S(2)}) async-start(), calls=%async_computation.2 | async-start | bytes 11943936
  44.9 1.3 copy-start.2
  45.0 844.5 %reduce-scatter.9.cloned.1.call-start = ((), (), s32[]{:S(2)}) async-start(), calls=%async_computation.3 | async-start | bytes 36495360
  134.2 6.8 copy-start.1
  135.9 3.3 collective-permute-start
  146.2 64.4 %copy-start = (bf16[1,2,1296,512]{2,3,1,0:T(8,128)(2,1)S(1)}, bf16[1,2,1296,512]{2,3,1,0:T(8,128)(2,1)}, u32[]{:S(2)}) copy-start(bf16[1,2,1296,512]{2,3,1,0:T(8,128)(2,1)} %get-tuple-element.5) | copy-start | bytes 7962628
  146.2 59.9 %collective-permute-start.1 = (bf16[2,1296,512]{2,1,0:T(8,128)(2,1)}, bf16[2,1296,512]{2,1,0:T(8,128)(2,1)}, u32[]{:S(2)}, u32[]{:S(2)}) collective-permute-start(bf16[2,1296,512]{2,1,0:T(8,128)(2,1)} %copy.13), channel_id=1, source_target_pairs={{0,2},{1,3},{2,0},{3,1},{4,6},{5,7},{6,4},{7,5},{8,10},{9,11},{10,... | collective-permute-start | bytes 7962632 | tf_op jit(solution)/shard_map/ppermute | solution.py:19
  224.8 115.9 %collective-permute-start.2 = (bf16[4,1296,512]{2,1,0:T(8,128)(2,1)}, bf16[4,1296,512]{2,1,0:T(8,128)(2,1)}, u32[]{:S(2)}, u32[]{:S(2)}) collective-permute-start(bf16[4,1296,512]{2,1,0:T(8,128)(2,1)} %bitcast.20), channel_id=1, source_target_pairs={{0,4},{1,5},{2,6},{3,7},{4,0},{5,1},{6,2},{7,3},{8,12},{9,13},{10,... | collective-permute-start | bytes 15925256 | tf_op jit(solution)/shard_map/ppermute | solution.py:19
  346.2 5.4 copy-start.3
  346.3 5.3 copy-start.4
Sparse Core Ops, SparseCore 0:
  45.1 85.3 reduce-scatter.6
  410.1 479.3 reduce-scatter.8
